TPU v7x, 32 devices: a whole 2x2x4 slice. The times are simulated.
32 devices in a mesh: seq: 16 (over z, y, core), mp: 2 (over x).
Axes of the slice: x: 2, y: 2, z: 4, core: 2. Of those that a mesh axis runs over, the one named last changes fastest.
Arguments:
- shared_qk: bfloat16 [2048, 4096], P('seq', 'mp'), may hold values from -40 to 40
- values: bfloat16 [2048, 4096], P('seq', 'mp'), may hold values from -6 to 6
- buckets: int32 [2048, 32], P('seq', 'mp'), may hold values from 0 to 15, as said below
- counts: int32 [16, 32, 16], P(None, 'mp'), may hold values from 0 to 16, as said below
- w_out: bfloat16 [4096, 4096], P('mp'), may hold values from -0.09375 to 0.09375
Outputs:
- projected: bfloat16 [2048, 4096], P('seq', 'mp')
Inputs may be any that keep to these rules, and one draw needn't show every extreme that they name: `buckets`: in each head at most 16 tokens among rows d * 128 to (d + 1) * 128 - 1 name one bucket, and in each head one bucket is named by exactly 16 tokens of every such group of rows. counts[d, h, b] is the number of rows among d * 128 to (d + 1) * 128 - 1 whose bucket in head h is b.
All inputs are finite; a program needn't handle non-finite values.
Results may differ from a plain program's by a relative error of at most 0.0057.
Values may be sent and summed in bfloat16 or wider, within the bound.
No kernel may reach another device: no remote copies, remote signals or barrier semaphores. Data moves between devices by JAX's collectives and lax.ppermute only.
A program may use at most 64 MiB of HBM per device.

v0:
```python
import math

import jax
import jax.numpy as jnp
from jax import lax
from jax.sharding import PartitionSpec as P

BLOCK = 256


SELF_SCORE = -100000.0


def passed_along(shard, axis, by):
    devices = lax.axis_size(axis)
    return lax.ppermute(shard, axis, [(i, (i + by) % devices) for i in range(devices)])


def block_attention(queries, window, window_live):
    head_dim = queries.shape[-1]
    block_rows = queries.shape[-2]
    key_rows = window[..., :head_dim]
    value_rows = window[..., head_dim:]
    scores = jnp.einsum("cqd,ckd->cqk", queries, key_rows, preferred_element_type=jnp.float32) * (
        1.0 / math.sqrt(head_dim)
    )
    query_place = jnp.arange(block_rows)[:, None] + block_rows
    key_place = jnp.arange(2 * block_rows)[None, :]
    itself = query_place == key_place
    scores = jnp.where(itself[None], SELF_SCORE, scores)
    allowed = window_live[:, None, :] | itself[None]
    row_max = jnp.max(jnp.where(allowed, scores, -1e30), axis=-1, keepdims=True)
    exp_terms = jnp.where(allowed, jnp.exp(scores - row_max), 0.0)
    weights = (exp_terms / jnp.sum(exp_terms, axis=-1, keepdims=True)).astype(jnp.bfloat16)
    attended = jnp.einsum("cqk,ckd->cqd", weights, value_rows, preferred_element_type=jnp.float32)
    return attended.astype(jnp.bfloat16)


def owner_layout(received, column, slot_count):
    source_count = column.shape[0]
    head_count = column.shape[1]
    upto_count = jnp.cumsum(column, axis=0)
    before_count = upto_count - column
    bucket_total = upto_count[-1]
    slot_range = jnp.arange(slot_count)
    source_dev = jnp.sum(upto_count[:, :, None] <= slot_range[None, None, :], axis=0)
    source_dev = jnp.minimum(source_dev, source_count - 1)
    source_range = jnp.arange(source_count)
    source_start = jnp.sum(
        jnp.where(source_dev[None] == source_range[:, None, None], before_count[:, :, None], 0),
        axis=0,
    )
    entry_row = jnp.clip(slot_range[None, :] - source_start, 0, received.shape[2] - 1)
    head_range = jnp.arange(head_count)
    layout = received[source_dev, head_range[:, None], entry_row]
    live = slot_range[None, :] < bucket_total[:, None]
    layout = jnp.where(live[..., None], layout, jnp.zeros((), layout.dtype))
    return (layout, live, before_count, bucket_total)


def tail_live(bucket_total, block_rows):
    return bucket_total[:, None] - block_rows + jnp.arange(block_rows)[None, :] >= 0


def last_rows(layout, bucket_total, block_rows):
    rank_index = bucket_total[:, None] - block_rows + jnp.arange(block_rows)[None, :]
    head_range = jnp.arange(layout.shape[0])
    rows = layout[head_range[:, None], jnp.maximum(rank_index, 0)]
    return jnp.where((rank_index >= 0)[..., None], rows, jnp.zeros((), rows.dtype))


def local(shared_qk, values, buckets, counts, w_out):
    tok_rows = shared_qk.shape[0]
    head_count = buckets.shape[1]
    head_dim = shared_qk.shape[1] // head_count
    seq_count = lax.axis_size("seq")
    capacity = 2 * tok_rows // seq_count
    slot_count = seq_count * capacity
    block_rows = BLOCK
    block_count = slot_count // block_rows
    own_index = lax.axis_index("seq")
    prev_index = (own_index + seq_count - 1) % seq_count
    head_range = jnp.arange(head_count)
    bucket_heads = buckets.T
    positions = jnp.arange(tok_rows)
    earlier = positions[None, :] < positions[:, None]
    same_bucket = bucket_heads[:, :, None] == bucket_heads[:, None, :]
    within = jnp.sum(same_bucket & earlier[None], axis=2)
    own_counts = lax.dynamic_index_in_dim(counts, own_index, 0, keepdims=False)
    own_starts = jnp.cumsum(own_counts, axis=1) - own_counts
    bucket_range = jnp.arange(seq_count)
    one_hot = bucket_heads[:, :, None] == bucket_range[None, None, :]
    token_start = jnp.sum(jnp.where(one_hot, own_starts[:, None, :], 0), axis=2)
    sorted_pos = token_start + within
    token_order = jnp.sum(
        jnp.where(sorted_pos[:, :, None] == positions[None, None, :], positions[None, :, None], 0),
        axis=1,
    )
    slot_range = jnp.arange(capacity)
    send_index = own_starts.T[:, :, None] + slot_range[None, None, :]
    filled = slot_range[None, None, :] < own_counts.T[:, :, None]
    token_pick = token_order[head_range[None, :, None], jnp.minimum(send_index, tok_rows - 1)]
    packed = jnp.concatenate(
        [
            shared_qk.reshape(tok_rows, head_count, head_dim),
            values.reshape(tok_rows, head_count, head_dim),
        ],
        axis=2,
    )
    outgoing = packed[token_pick, head_range[None, :, None]]
    outgoing = jnp.where(filled[..., None], outgoing, jnp.zeros((), outgoing.dtype))
    own_column = lax.dynamic_index_in_dim(counts, own_index, 2, keepdims=False)
    prev_column = lax.dynamic_index_in_dim(counts, prev_index, 2, keepdims=False)
    prev_total = jnp.sum(prev_column, axis=0)
    received = lax.all_to_all(outgoing, "seq", split_axis=0, concat_axis=0, tiled=True)
    layout, live, before_count, bucket_total = owner_layout(received, own_column, slot_count)
    tail_rows = last_rows(layout, bucket_total, block_rows)
    prev_rows = passed_along(tail_rows, "seq", 1)
    prev_live = tail_live(prev_total, block_rows)
    keys_all = jnp.concatenate([prev_rows, layout], axis=1)
    live_all = jnp.concatenate([prev_live, live], axis=1)
    window = jnp.concatenate(
        [
            keys_all[:, :slot_count].reshape(head_count, block_count, block_rows, 2 * head_dim),
            keys_all[:, block_rows:].reshape(head_count, block_count, block_rows, 2 * head_dim),
        ],
        axis=2,
    )
    window_live = jnp.concatenate(
        [
            live_all[:, :slot_count].reshape(head_count, block_count, block_rows),
            live_all[:, block_rows:].reshape(head_count, block_count, block_rows),
        ],
        axis=2,
    )
    queries = layout[..., :head_dim].reshape(head_count, block_count, block_rows, head_dim)
    attended = lax.map(
        lambda per_head: block_attention(per_head[0], per_head[1], per_head[2]),
        (queries, window, window_live),
    )
    out_layout = attended.reshape(head_count, slot_count, head_dim)
    back_index = before_count[:, :, None] + slot_range[None, None, :]
    back_filled = slot_range[None, None, :] < own_column[:, :, None]
    back_rows = out_layout[head_range[None, :, None], jnp.minimum(back_index, slot_count - 1)]
    back_rows = jnp.where(back_filled[..., None], back_rows, jnp.zeros((), back_rows.dtype))
    returned = lax.all_to_all(back_rows, "seq", split_axis=0, concat_axis=0, tiled=True)
    token_out = returned[buckets, head_range[None, :], within.T]
    token_out = token_out.reshape(tok_rows, head_count * head_dim)
    partial_sum = jnp.dot(token_out, w_out, preferred_element_type=jnp.float32)
    projected = lax.psum_scatter(partial_sum, "mp", scatter_dimension=1, tiled=True)
    return projected.astype(jnp.bfloat16)


def solution(mesh):
    placed = (P("seq", "mp"), P("seq", "mp"), P("seq", "mp"), P(None, "mp", None), P("mp", None))
    return jax.shard_map(
        local, mesh=mesh, in_specs=placed, out_specs=P("seq", "mp"), check_vma=False
    )
```

profile of v0, /device:TPU:0, one launch (start us, length us, event | category | flops | bytes accessed | tf_op | source)
XLA Modules:
  0.0 400.5 jit_solution(6937091656879628295)
XLA Ops:
  8.3 1.4 convert_reduce_fusion
  10.4 25.6 %gather_fusion = s32[4096]{0:T(1024)S(1)} fusion(s32[16,128]{1,0:T(8,128)S(1)} %select_reduce_fusion.1, s32[4096]{0:T(1024)S(1)} %reshape.373), kind=kCustom, calls=%fused_computation | custom fusion | bytes 65536 | tf_op jit(solution)/shard_map/gather | solution.py:102
  36.8 21.6 %gather_fusion.1 = bf16[4096,256]{1,0:T(8,128)(2,1)S(1)} fusion(bf16[128,16,256]{2,1,0:T(8,128)(2,1)S(1)} %pad_maximum_fusion, s32[4096]{0:T(1024)S(1)} %reshape.379), kind=kCustom, calls=%fused_computation.1 | custom fusion | bytes 4227072 | tf_op jit(solution)/shard_map/gather | solution.py:110
  58.4 1.7 broadcast_select_fusion.2
  60.1 7.5 %all-to-all-start = ((bf16[16,16,16,256]{3,2,1,0:T(8,128)(2,1)}), bf16[16,16,16,256]{3,2,1,0:T(8,128)(2,1)S(1)}, u32[]{:S(2)}, u32[]{:S(2)}) async-start(bf16[16,16,16,256]{3,2,1,0:T(8,128)(2,1)} %broadcast_select_fusion.2), calls=%async_computation | async-start | bytes 4194304 | tf_op jit(solution)/shard_map/all_to_all | solution.py:115
  68.7 40.0 %all-to-all-done = bf16[16,16,16,256]{3,2,1,0:T(8,128)(2,1)S(1)} async-done(((bf16[16,16,16,256]{3,2,1,0:T(8,128)(2,1)}), bf16[16,16,16,256]{3,2,1,0:T(8,128)(2,1)S(1)}, u32[]{:S(2)}, u32[]{:S(2)}) %all-to-all-start) | async-done | bytes 2097184 | tf_op jit(solution)/shard_map/all_to_all | solution.py:115
  108.7 45.3 %gather_fusion.2 = bf16[4096,256]{1,0:T(8,128)(2,1)} fusion(bf16[16,16,16,256]{3,2,1,0:T(8,128)(2,1)S(1)} %all-to-all-done, s32[4096]{0:T(1024)S(1)} %bitcast.112), kind=kCustom, calls=%fused_computation.2 | custom fusion | bytes 4243456 | tf_op jit(solution)/shard_map/gather | solution.py:55
  154.0 1.9 broadcast_select_fusion.3
  155.9 40.7 %gather_fusion.3 = bf16[4096,256]{1,0:T(8,128)(2,1)} fusion(bf16[16,256,256]{2,1,0:T(8,128)(2,1)S(1)} %broadcast_select_fusion.3, s32[4096]{0:T(1024)S(1)} %bitcast.113), kind=kCustom, calls=%fused_computation.3 | custom fusion | bytes 4227072 | tf_op jit(solution)/shard_map/gather | solution.py:68
  196.6 2.9 broadcast_select_fusion.1
  203.6 29.9 %collective-permute-done = bf16[16,256,256]{2,1,0:T(8,128)(2,1)} collective-permute-done((bf16[16,256,256]{2,1,0:T(8,128)(2,1)}, bf16[16,256,256]{2,1,0:T(8,128)(2,1)}, u32[]{:S(2)}, u32[]{:S(2)}) %collective-permute-start) | collective-permute-done | bytes 2097184 | tf_op jit(solution)/shard_map/ppermute | solution.py:16
  233.4 3.9 maximum_bitcast_fusion
  237.3 47.1 %while.10 = (s32[]{:T(128)}, bf16[16,1,256,128]{3,2,1,0:T(8,128)(2,1)S(1)}, pred[16,1,512]{2,0,1:T(8,128)(4,1)S(1)}, bf16[16,1,256,128]{3,2,1,0:T(8,128)(2,1)}, bf16[16,1,512,256]{3,2,1,0:T(8,128)(2,1)}, /*index=5*/s32[]{:T(128)}) while((s32[]{:T(128)}, bf16[16,1,256,128]{3,2,1,0:T(8,128)(2,1)S(1)}, pred[16,1,512]{2,0,1:T(8,128)(4,1)S(1)}, ...), condition=%wide.region_11.12_spmd, body=%wide.region_8.11_spmd.sunk | while | flops 69369600 | bytes 2502737 | solution.py:137
  238.3 1.2 select_reduce_fusion.5
  241.3 1.2 select_reduce_fusion.5
  247.1 1.2 select_reduce_fusion.5
  250.1 1.2 select_reduce_fusion.5
  253.0 1.2 select_reduce_fusion.5
  256.0 1.2 select_reduce_fusion.5
  258.9 1.2 select_reduce_fusion.5
  264.8 1.2 select_reduce_fusion.5
  270.7 1.2 select_reduce_fusion.5
  276.6 1.2 select_reduce_fusion.5
  282.5 1.2 select_reduce_fusion.5
  284.4 21.7 %gather_fusion.4 = bf16[4096,128]{1,0:T(8,128)(2,1)S(1)} fusion(bf16[16,256,128]{2,1,0:T(8,128)(2,1)S(1)} %bitcast.114, s32[4096]{0:T(1024)S(1)} %reshape.397), kind=kCustom, calls=%fused_computation.4 | custom fusion | bytes 2129920 | tf_op jit(solution)/shard_map/gather | solution.py:144
  306.2 1.5 broadcast_select_fusion.4
  307.7 3.7 all-to-all-start.1
  311.8 22.4 %all-to-all-done.1 = bf16[16,16,16,128]{3,2,1,0:T(8,128)(2,1)S(1)} async-done(((bf16[16,16,16,128]{3,2,1,0:T(8,128)(2,1)}), bf16[16,16,16,128]{3,2,1,0:T(8,128)(2,1)S(1)}, u32[]{:S(2)}, u32[]{:S(2)}) %all-to-all-start.1) | async-done | bytes 1048608 | tf_op jit(solution)/shard_map/all_to_all | solution.py:146
  334.2 13.4 %gather_fusion.5 = bf16[2048,128]{1,0:T(8,128)(2,1)S(1)} fusion(bf16[16,16,16,128]{3,2,1,0:T(8,128)(2,1)S(1)} %all-to-all-done.1, s32[2048]{0:T(1024)S(1)} %reshape.403), kind=kCustom, calls=%fused_computation.5 | custom fusion | bytes 1073152 | tf_op jit(solution)/shard_map/gather | solution.py:147
  347.8 9.5 %fusion.41 = f32[128,4096]{1,0:T(8,128)} fusion(bf16[128,2048]{1,0:T(8,128)(2,1)S(1)} %reshape.372, bf16[2048,4096]{1,0:T(8,128)(2,1)} %param.11), kind=kOutput, calls=%fused_computation.103 | convolution fusion | flops 2147483648 | bytes 19398656 | tf_op jit(solution)/shard_map/dot_general | solution.py:149
  357.3 34.2 %reduce-scatter.2.cloned.1.call-done = f32[128,2048]{1,0:T(8,128)} async-done(((f32[128,4096]{1,0:T(8,128)}), f32[128,2048]{1,0:T(8,128)}) %reduce-scatter.2.cloned.1.call-update) | async-done | bytes 1048592 | tf_op jit(solution)/shard_map/reduce_scatter | solution.py:150
  391.5 2.1 convert_element_type.19
  (144 shorter events, 42.1 us)
Async XLA Ops:
  10.3 25.9 %copy-start.2 = (bf16[128,2048]{1,0:T(8,128)(2,1)S(1)}, bf16[128,2048]{1,0:T(8,128)(2,1)}, u32[]{:S(2)}) copy-start(bf16[128,2048]{1,0:T(8,128)(2,1)} %param.7) | copy-start | bytes 1572868
  10.3 26.0 %copy-start.3 = (bf16[128,2048]{1,0:T(8,128)(2,1)S(1)}, bf16[128,2048]{1,0:T(8,128)(2,1)}, u32[]{:S(2)}) copy-start(bf16[128,2048]{1,0:T(8,128)(2,1)} %param.8) | copy-start | bytes 1572868
  60.1 7.6 %copy-start.1 = (s32[16,16,16]{2,1,0:T(8,128)S(1)}, s32[16,16,16]{2,1,0:T(8,128)}, u32[]{:S(2)}) copy-start(s32[16,16,16]{2,1,0:T(8,128)} %param.10) | copy-start | bytes 49156
  60.1 48.5 %all-to-all-start = ((bf16[16,16,16,256]{3,2,1,0:T(8,128)(2,1)}), bf16[16,16,16,256]{3,2,1,0:T(8,128)(2,1)S(1)}, u32[]{:S(2)}, u32[]{:S(2)}) async-start(bf16[16,16,16,256]{3,2,1,0:T(8,128)(2,1)} %broadcast_select_fusion.2), calls=%async_computation | async-start | bytes 4194304 | tf_op jit(solution)/shard_map/all_to_all | solution.py:115
  199.5 33.9 %collective-permute-start = (bf16[16,256,256]{2,1,0:T(8,128)(2,1)}, bf16[16,256,256]{2,1,0:T(8,128)(2,1)}, u32[]{:S(2)}, u32[]{:S(2)}) collective-permute-start(bf16[16,256,256]{2,1,0:T(8,128)(2,1)} %broadcast_select_fusion.1), channel_id=1, source_target_pairs={{0,2},{2,4},{4,6},{6,8},{8,10},{10,12},{12,14},{14,16},{16,18},{18... | collective-permute-start | bytes 6291464 | tf_op jit(solution)/shard_map/ppermute | solution.py:16
  200.7 2.0 copy-start
  306.2 5.4 %copy-start.4 = (s32[128,16]{0,1:T(8,128)S(1)}, s32[128,16]{0,1:T(8,128)}, u32[]{:S(2)}) copy-start(s32[128,16]{0,1:T(8,128)} %param.9) | copy-start | bytes 24580
  307.7 26.5 %all-to-all-start.1 = ((bf16[16,16,16,128]{3,2,1,0:T(8,128)(2,1)}), bf16[16,16,16,128]{3,2,1,0:T(8,128)(2,1)S(1)}, u32[]{:S(2)}, u32[]{:S(2)}) async-start(bf16[16,16,16,128]{3,2,1,0:T(8,128)(2,1)} %broadcast_select_fusion.4), calls=%async_computation.1 | async-start | bytes 2097152 | tf_op jit(solution)/shard_map/all_to_all | solution.py:146
  311.4 80.2 %reduce-scatter.2.cloned.1.call-start = ((), (), s32[]{:S(2)}) async-start(), calls=%async_computation.3 | async-start | bytes 3145728 | tf_op jit(solution)/shard_map/reduce_scatter | solution.py:150
Sparse Core Ops, SparseCore 0:
  357.5 34.0 reduce-scatter.1
where the time goes:
time: 402 us; the launch traced here: 400 us
  local copies, waits for them, and re-layouts  188 us (47%)
  waiting for transfers between devices  126 us (31%)
  matrix products  35 us (9%)
  other arithmetic  24.3 us (6%)
  between operations  13.8 us (3%)
  starting transfers between devices  12.4 us (3%)
    gather x1, local copies, waits for them, and re-layouts, owner_layout(): layout = received[source_dev, head_range[:, None], entry_row]  45.3 us
    gather x1, local copies, waits for them, and re-layouts, last_rows(): rows = layout[head_range[:, None], jnp.maximum(rank_index, 0)]  40.7 us
    all_to_all x1, waiting for transfers between devices, local(): lax.all_to_all(outgoing, 'seq', split_axis=0, concat_axis=0, tiled=True)  40 us
    reduce_scatter x1, waiting for transfers between devices, local(): lax.psum_scatter(partial_sum, 'mp', scatter_dimension=1, tiled=True)  34.2 us
    ppermute x1, waiting for transfers between devices, passed_along(): lax.ppermute(shard, axis, [(i, (i + by) % devices) for i in range(devices)])  29.9 us
    gather x2, local copies, waits for them, and re-layouts, local(): token_order[head_range[None, :, None], jnp.minimum(send_index, tok_rows -...  25.7 us
    all_to_all x1, waiting for transfers between devices, local(): lax.all_to_all(back_rows, 'seq', split_axis=0, concat_axis=0, tiled=True)  22.4 us
    gather x1, local copies, waits for them, and re-layouts, local(): out_layout[head_range[None, :, None], jnp.minimum(back_index, slot_count...  21.7 us
  transfers between devices with their start and end apart: 4, of which 4 were waited for; matrix products, arithmetic and copies ran while one was open for 1% of the time, Pallas kernels for 0%

commit v1 on v0

--- a/solution.py
+++ b/solution.py
@@ -1,11 +1,15 @@
+import functools
 import math
 
 import jax
 import jax.numpy as jnp
 from jax import lax
+from jax.experimental import pallas as pl
+from jax.experimental.pallas import tpu as pltpu
 from jax.sharding import PartitionSpec as P
 
 BLOCK = 256
+MASKED = -1e30
 
 
 SELF_SCORE = -100000.0
@@ -69,7 +73,7 @@
     return jnp.where((rank_index >= 0)[..., None], rows, jnp.zeros((), rows.dtype))
 
 
-def local(shared_qk, values, buckets, counts, w_out):
+def local_by_bucket(shared_qk, values, buckets, counts, w_out):
     tok_rows = shared_qk.shape[0]
     head_count = buckets.shape[1]
     head_dim = shared_qk.shape[1] // head_count
@@ -151,6 +155,161 @@
     return projected.astype(jnp.bfloat16)
 
 
+def weights_kernel(bucket_ref, qk_ref, out_ref, query_ref, key_ref, score_ref, *, bucket_count, query_rows):
+    source_count, tok_rows = bucket_ref.shape
+    head_dim = qk_ref.shape[1]
+    token_count = qk_ref.shape[0]
+    lanes = query_ref.shape[1] - head_dim
+    lane = lax.broadcasted_iota(jnp.int32, (tok_rows, lanes), 1)
+    query_ref[:, :head_dim] = qk_ref[...]
+    key_ref[:, :head_dim] = qk_ref[...]
+    for source in range(source_count):
+        rows = slice(source * tok_rows, (source + 1) * tok_rows)
+        row = bucket_ref[source : source + 1, :].astype(jnp.float32)
+        bucket = jnp.broadcast_to(row, (lanes, tok_rows)).T.astype(jnp.int32)
+        following = jnp.where(bucket == bucket_count - 1, 0, bucket + 1)
+        own = lane == bucket
+        query_ref[rows, head_dim:] = jnp.where(own, 1.0, 0.0).astype(query_ref.dtype)
+        key_ref[rows, head_dim:] = jnp.where(own | (lane == following), 0.0, MASKED).astype(key_ref.dtype)
+    scale = 1.0 / math.sqrt(head_dim)
+    strip = 16
+
+    def one_block(block, carry):
+        start = pl.multiple_of(block * query_rows, query_rows)
+        score_ref[...] = lax.dot_general(
+            query_ref[pl.ds(start, query_rows), :],
+            key_ref[...],
+            (((1,), (1,)), ((), ())),
+            preferred_element_type=jnp.float32,
+        )
+        square = (query_rows, query_rows)
+        itself = lax.broadcasted_iota(jnp.int32, square, 0) == lax.broadcasted_iota(jnp.int32, square, 1)
+        own_columns = score_ref[:, pl.ds(start, query_rows)]
+        score_ref[:, pl.ds(start, query_rows)] = jnp.where(itself, SELF_SCORE / scale, own_columns)
+        for at in range(0, query_rows, strip):
+            scores = score_ref[at : at + strip, :]
+            row_max = jnp.max(scores, axis=1, keepdims=True)
+            exp_terms = jnp.exp((scores - row_max) * scale)
+            inverse = 1.0 / jnp.sum(exp_terms, axis=1, keepdims=True)
+            out_ref[pl.ds(start + at, strip), :] = (exp_terms * inverse).astype(out_ref.dtype)
+        return carry
+
+    lax.fori_loop(0, token_count // query_rows, one_block, 0)
+
+
+def head_weights(bucket, qk, bucket_count):
+    token_count, head_dim = qk.shape
+    lanes = 128
+    query_rows = min(256, token_count)
+    return pl.pallas_call(
+        functools.partial(weights_kernel, bucket_count=bucket_count, query_rows=query_rows),
+        out_shape=jax.ShapeDtypeStruct((token_count, token_count), qk.dtype),
+        scratch_shapes=[
+            pltpu.VMEM((token_count, head_dim + lanes), qk.dtype),
+            pltpu.VMEM((token_count, head_dim + lanes), qk.dtype),
+            pltpu.VMEM((query_rows, token_count), jnp.float32),
+        ],
+        name="head_weights",
+    )(bucket, qk)
+
+
+def attend_kernel(weight_ref, value_ref, out_ref):
+    out_ref[...] = jnp.dot(
+        weight_ref[...], value_ref[...], preferred_element_type=jnp.float32
+    ).astype(out_ref.dtype)
+
+
+def head_attend(weights, value):
+    token_count, head_dim = value.shape
+    rows = min(512, token_count)
+    return pl.pallas_call(
+        attend_kernel,
+        grid=(token_count // rows,),
+        in_specs=[
+            pl.BlockSpec((rows, token_count), lambda i: (i, 0)),
+            pl.BlockSpec((token_count, head_dim), lambda i: (0, 0)),
+        ],
+        out_specs=pl.BlockSpec((rows, head_dim), lambda i: (i, 0)),
+        out_shape=jax.ShapeDtypeStruct((token_count, head_dim), value.dtype),
+        name="head_attend",
+    )(weights, value)
+
+
+def project_kernel(part_ref, token_ref, w_ref, out_ref, wide_ref):
+    head_count, tok_rows, head_dim = token_ref.shape
+
+    @pl.when(pl.program_id(0) == 0)
+    def _():
+        for head in range(head_count):
+            wide_ref[:, head * head_dim : (head + 1) * head_dim] = token_ref[head]
+
+    out_ref[...] = jnp.dot(
+        wide_ref[...], w_ref[...], preferred_element_type=jnp.float32
+    ).astype(out_ref.dtype)
+
+
+def project_part(token_heads, w_out, part, part_count, dtype):
+    head_count, tok_rows, head_dim = token_heads.shape
+    depth, features = w_out.shape
+    width = features // part_count
+    columns = min(512, width)
+    steps = width // columns
+    return pl.pallas_call(
+        project_kernel,
+        grid_spec=pltpu.PrefetchScalarGridSpec(
+            num_scalar_prefetch=1,
+            grid=(steps,),
+            in_specs=[
+                pl.BlockSpec((head_count, tok_rows, head_dim), lambda j, part_ref: (0, 0, 0)),
+                pl.BlockSpec((depth, columns), lambda j, part_ref: (0, part_ref[0] * steps + j)),
+            ],
+            out_specs=pl.BlockSpec((tok_rows, columns), lambda j, part_ref: (0, j)),
+            scratch_shapes=[pltpu.VMEM((tok_rows, depth), token_heads.dtype)],
+        ),
+        out_shape=jax.ShapeDtypeStruct((tok_rows, width), dtype),
+        name="project_part",
+    )(jnp.reshape(part, (1,)), token_heads, w_out)
+
+
+def to_heads(shard, head_dim, seq_count):
+    tok_rows = shard.shape[0]
+    by_head = jnp.transpose(shard.reshape(tok_rows, seq_count, head_dim), (1, 0, 2))
+    return lax.all_to_all(by_head, "seq", split_axis=0, concat_axis=0, tiled=True)
+
+
+def local_by_head(shared_qk, values, buckets, counts, w_out):
+    tok_rows = shared_qk.shape[0]
+    head_count = buckets.shape[1]
+    head_dim = shared_qk.shape[1] // head_count
+    seq_count = lax.axis_size("seq")
+    part_count = lax.axis_size("mp")
+    token_count = tok_rows * seq_count
+    bucket_count = counts.shape[2]
+    head_buckets = lax.all_to_all(buckets.T, "seq", split_axis=0, concat_axis=0, tiled=True)
+    head_qk = to_heads(shared_qk, head_dim, seq_count)
+    head_qk, values = lax.optimization_barrier((head_qk, values))
+    head_values = to_heads(values, head_dim, seq_count)
+    weights = head_weights(head_buckets, head_qk.reshape(token_count, head_dim), bucket_count)
+    attended = head_attend(weights, head_values.reshape(token_count, head_dim))
+    token_heads = lax.all_to_all(
+        attended.reshape(seq_count, tok_rows, head_dim), "seq", split_axis=0, concat_axis=0, tiled=True
+    )
+    part = lax.axis_index("mp")
+    theirs = project_part(token_heads, w_out, 1 - part, part_count, jnp.bfloat16)
+    arrived = lax.ppermute(theirs, "mp", [(0, 1), (1, 0)])
+    ours = project_part(token_heads, w_out, part, part_count, jnp.float32)
+    return (ours + arrived.astype(jnp.float32)).astype(jnp.bfloat16)
+
+
+def local(shared_qk, values, buckets, counts, w_out):
+    head_count = buckets.shape[1]
+    seq_count = lax.axis_size("seq")
+    one_head_each = head_count == seq_count and counts.shape[2] == seq_count and 2 < seq_count <= 128
+    if one_head_each and lax.axis_size("mp") == 2 and 2 * shared_qk.shape[0] <= BLOCK:
+        return local_by_head(shared_qk, values, buckets, counts, w_out)
+    return local_by_bucket(shared_qk, values, buckets, counts, w_out)
+
+
 def solution(mesh):
     placed = (P("seq", "mp"), P("seq", "mp"), P("seq", "mp"), P(None, "mp", None), P("mp", None))
     return jax.shard_map(

time: 402 us -> 101 us (0.25)
  local copies, waits for them, and re-layouts: 188 us -> 4.73 us
  waiting for transfers between devices: 126 us -> 26.2 us
  matrix products: 35 us -> 0 us
  Pallas kernels: 0 us -> 31.5 us
  other arithmetic: 24.3 us -> 2.13 us
  blocking collectives: 0 us -> 21.6 us
  between operations: 13.8 us -> 0.05 us
    gather x7 -> x0, local copies, waits for them, and re-layouts: 168 us -> none  [the longest x1 45.3 us: owner_layout(): layout = received[source_dev, head_range[:, None], entry_row]]
    all_to_all x2 -> x3, waiting for transfers between devices: 62.4 us -> 19.5 us  [the longest x1 14.3 us: local_by_head(): lax.all_to_all(attended.reshape(seq_count, tok_rows, head_dim), 'seq', sp...]
    dot_general x33 -> x0, matrix products: 35 us -> none  [the longest x16 19.3 us: block_attention(): jnp.einsum('cqd,ckd->cqk', queries, key_rows, preferred_element_type=jnp....]
    reduce_scatter x1 -> x0, waiting for transfers between devices: 34.2 us -> none  [local(): lax.psum_scatter(partial_sum, 'mp', scatter_dimension=1, tiled=True)]
    pallas_call x0 -> x4, Pallas kernels: none -> 31.5 us  [the longest x1 13.4 us: head_weights(): pl.pallas_call(functools.partial(weights_kernel, bucket_count=bucket_coun...]
    ppermute x1, waiting for transfers between devices: 29.9 us -> 6.68 us  [local_by_head(): arrived = lax.ppermute(theirs, 'mp', [(0, 1), (1, 0)])]
    all_to_all x0 -> x1, blocking collectives: none -> 21.6 us  [to_heads(): lax.all_to_all(by_head, 'seq', split_axis=0, concat_axis=0, tiled=True)]
    squeeze x16 -> x0, local copies, waits for them, and re-layouts: 15.5 us -> none  [local(): lax.map(lambda per_head: block_attention(per_head[0], per_head[1], per_he...]
  transfers between devices with their start and end apart: 4 -> 4, of which waited for: 4 -> 4; matrix products, arithmetic and copies ran while one was open for 1% -> 2% of each run, Pallas kernels for 0% -> 19%
where the time goes in v1:
time: 101 us
  Pallas kernels  31.5 us (31%)
  waiting for transfers between devices  26.2 us (26%)
  blocking collectives  21.6 us (21%)
  starting transfers between devices  14.3 us (14%)
  local copies, waits for them, and re-layouts  4.73 us (5%)
  other arithmetic  2.13 us (2%)
    all_to_all x1, blocking collectives, to_heads(): lax.all_to_all(by_head, 'seq', split_axis=0, concat_axis=0, tiled=True)  21.6 us
    all_to_all x1, waiting for transfers between devices, local_by_head(): lax.all_to_all(attended.reshape(seq_count, tok_rows, head_dim), 'seq', sp...  14.3 us
    pallas_call x1, Pallas kernels, head_weights(): pl.pallas_call(functools.partial(weights_kernel, bucket_count=bucket_coun...  13.4 us
    pallas_call x2, Pallas kernels, project_part(): pl.pallas_call(project_kernel, grid_spec=pltpu.PrefetchScalarGridSpec(num...  11.9 us
    ppermute x1, waiting for transfers between devices, local_by_head(): arrived = lax.ppermute(theirs, 'mp', [(0, 1), (1, 0)])  6.68 us
    pallas_call x1, Pallas kernels, head_attend(): pl.pallas_call(attend_kernel, grid=(token_count // rows,), in_specs=[pl.B...  6.27 us
    all_to_all x1, starting transfers between devices, local_by_head(): lax.all_to_all(attended.reshape(seq_count, tok_rows, head_dim), 'seq', sp...  5.1 us
    all_to_all x1, waiting for transfers between devices, local_by_head(): lax.all_to_all(buckets.T, 'seq', split_axis=0, concat_axis=0, tiled=True)  4.39 us
  transfers between devices with their start and end apart: 4, of which 4 were waited for; matrix products, arithmetic and copies ran while one was open for 2% of the time, Pallas kernels for 19%

profile of v1, /device:TPU:0, one launch (start us, length us, event | category | flops | bytes accessed | tf_op | source)
XLA Modules:
  0.0 100.5 jit_solution(4607179894554351535)
XLA Ops:
  0.0 0.0 copy-start
  0.0 1.0 %copy-done = bf16[128,2048]{1,0:T(8,128)(2,1)S(1)} copy-done((bf16[128,2048]{1,0:T(8,128)(2,1)S(1)}, bf16[128,2048]{1,0:T(8,128)(2,1)}, u32[]{:S(2)}) %copy-start) | copy-done | bytes 524312
  1.0 0.1 bitcast_bitcast_fusion.1
  1.2 21.6 %all_to_all.26 = bf16[16,128,128]{2,1,0:T(8,128)(2,1)} all-to-all(bf16[16,128,128]{2,1,0:T(8,128)(2,1)S(1)} %bitcast_bitcast_fusion.1), channel_id=1, replica_groups=mesh['seq'=16,'mp'=2] {'seq'}, dimensions={0} | all-to-all | bytes 1048576 | tf_op jit(solution)/shard_map/all_to_all | solution.py:277
  22.8 4.2 %all-to-all-start = ((s32[16,1,128]{2,1,0:T(1,128)}), s32[16,1,128]{2,1,0:T(1,128)S(1)}, u32[]{:S(2)}, u32[]{:S(2)}) async-start(s32[16,1,128]{2,1,0:T(1,128)} %bitcast.27), calls=%async_computation | async-start | bytes 16384 | tf_op jit(solution)/shard_map/all_to_all | solution.py:288
  26.9 2.0 %bitcast_bitcast_fusion = bf16[16,128,128]{2,1,0:T(8,128)(2,1)} fusion(bf16[128,2048]{1,0:T(8,128)(2,1)} %param.6), kind=kLoop, calls=%fused_computation.1 | loop fusion | bytes 1048576 | tf_op jit(solution)/shard_map/transpose | solution.py:276
  28.9 4.4 %all-to-all-done = s32[16,1,128]{2,1,0:T(1,128)S(1)} async-done(((s32[16,1,128]{2,1,0:T(1,128)}), s32[16,1,128]{2,1,0:T(1,128)S(1)}, u32[]{:S(2)}, u32[]{:S(2)}) %all-to-all-start) | async-done | bytes 8224 | tf_op jit(solution)/shard_map/all_to_all | solution.py:288
  33.3 0.0 copy-start.3
  33.3 3.6 %all-to-all-start.2 = ((bf16[16,128,128]{2,1,0:T(8,128)(2,1)}), bf16[16,128,128]{2,1,0:T(8,128)(2,1)S(1)}, u32[]{:S(2)}, u32[]{:S(2)}) async-start(bf16[16,128,128]{2,1,0:T(8,128)(2,1)} %bitcast_bitcast_fusion), calls=%async_computation.2 | async-start | bytes 1048576 | tf_op jit(solution)/shard_map/all_to_all | solution.py:277
  36.9 0.0 copy-done.3
  36.9 13.4 %head_weights.1.weight_ref = bf16[2048,2048]{1,0:T(8,128)(2,1)} custom-call(s32[16,128]{1,0:T(8,128)} %bitcast.26, bf16[2048,128]{1,0:T(8,128)(2,1)} %bitcast.23), custom_call_target="tpu_custom_call" | custom-call | tf_op jit(solution)/shard_map/head_weights/pallas_call | solution.py:204
  50.3 0.9 all-to-all-done.2
  51.1 0.0 copy-start.2
  51.1 0.8 copy-done.2
  51.9 6.3 %head_attend.1 = bf16[2048,128]{1,0:T(8,128)(2,1)} custom-call(bf16[2048,2048]{1,0:T(8,128)(2,1)} %head_weights.1.weight_ref, bf16[2048,128]{1,0:T(8,128)(2,1)} %bitcast.25), custom_call_target="tpu_custom_call" | custom-call | tf_op jit(solution)/shard_map/head_attend/pallas_call | solution.py:225
  58.2 5.1 %all-to-all-start.3 = ((bf16[16,128,128]{2,1,0:T(8,128)(2,1)}), bf16[16,128,128]{2,1,0:T(8,128)(2,1)S(1)}, u32[]{:S(2)}, u32[]{:S(2)}) async-start(bf16[16,128,128]{2,1,0:T(8,128)(2,1)} %bitcast.24), calls=%async_computation.3 | async-start | bytes 1048576 | tf_op jit(solution)/shard_map/all_to_all | solution.py:294
  63.3 14.3 %all-to-all-done.3.token_ref = bf16[16,128,128]{2,1,0:T(8,128)(2,1)S(1)} async-done(((bf16[16,128,128]{2,1,0:T(8,128)(2,1)}), bf16[16,128,128]{2,1,0:T(8,128)(2,1)S(1)}, u32[]{:S(2)}, u32[]{:S(2)}) %all-to-all-start.3) | async-done | bytes 524320 | tf_op jit(solution)/shard_map/all_to_all | solution.py:294
  77.6 0.0 copy-start.1
  77.6 0.8 copy-done.1
  78.4 5.9 %project_part.3 = bf16[128,2048]{1,0:T(8,128)(2,1)} custom-call(s32[1]{0:T(128)} %bitcast.9.part_ref, bf16[16,128,128]{2,1,0:T(8,128)(2,1)} %copy-done.1, bf16[2048,4096]{1,0:T(8,128)(2,1)} %w_ref.3), custom_call_target="tpu_custom_call" | custom-call | tf_op jit(solution)/shard_map/project_part/pallas_call | solution.py:257
  84.2 1.5 %collective-permute-start = (bf16[128,2048]{1,0:T(8,128)(2,1)}, bf16[128,2048]{1,0:T(8,128)(2,1)S(1)}, u32[]{:S(2)}, u32[]{:S(2)}) collective-permute-start(bf16[128,2048]{1,0:T(8,128)(2,1)} %project_part.3), channel_id=1, source_target_pairs={{0,1},{1,0},{2,3},{3,2},{4,5},{5,4},{6,7},{7,6},{8,9},{9,8},{10,11... | collective-permute-start | bytes 1572872 | tf_op jit(solution)/shard_map/ppermute | solution.py:299
  85.7 6.0 %project_part.2 = f32[128,2048]{1,0:T(8,128)} custom-call(s32[1]{0:T(128)} %bitcast.part_ref, bf16[16,128,128]{2,1,0:T(8,128)(2,1)} %copy-done.1, bf16[2048,4096]{1,0:T(8,128)(2,1)} %w_ref.3), custom_call_target="tpu_custom_call" | custom-call | tf_op jit(solution)/shard_map/project_part/pallas_call | solution.py:257
  91.7 6.7 %collective-permute-done = bf16[128,2048]{1,0:T(8,128)(2,1)S(1)} collective-permute-done((bf16[128,2048]{1,0:T(8,128)(2,1)}, bf16[128,2048]{1,0:T(8,128)(2,1)S(1)}, u32[]{:S(2)}, u32[]{:S(2)}) %collective-permute-start) | collective-permute-done | bytes 524320 | tf_op jit(solution)/shard_map/ppermute | solution.py:299
  98.4 2.1 %add_convert_fusion = bf16[128,2048]{1,0:T(8,128)(2,1)} fusion(f32[128,2048]{1,0:T(8,128)} %project_part.2, bf16[128,2048]{1,0:T(8,128)(2,1)S(1)} %collective-permute-done), kind=kLoop, calls=%fused_computation | loop fusion | flops 786432 | bytes 2097152 | tf_op jit(solution)/shard_map/convert_element_type | solution.py:301
Async XLA Ops:
  0.0 1.0 %copy-start = (bf16[128,2048]{1,0:T(8,128)(2,1)S(1)}, bf16[128,2048]{1,0:T(8,128)(2,1)}, u32[]{:S(2)}) copy-start(bf16[128,2048]{1,0:T(8,128)(2,1)} %param.5) | copy-start | bytes 1572868
  22.8 10.5 %all-to-all-start = ((s32[16,1,128]{2,1,0:T(1,128)}), s32[16,1,128]{2,1,0:T(1,128)S(1)}, u32[]{:S(2)}, u32[]{:S(2)}) async-start(s32[16,1,128]{2,1,0:T(1,128)} %bitcast.27), calls=%async_computation | async-start | bytes 16384 | tf_op jit(solution)/shard_map/all_to_all | solution.py:288
  33.3 3.6 %copy-start.3 = (s32[16,1,128]{2,1,0:T(1,128)}, s32[16,1,128]{2,1,0:T(1,128)S(1)}, u32[]{:S(2)}) copy-start(s32[16,1,128]{2,1,0:T(1,128)S(1)} %all-to-all-done) | copy-start | bytes 24580
  33.3 17.8 %all-to-all-start.2 = ((bf16[16,128,128]{2,1,0:T(8,128)(2,1)}), bf16[16,128,128]{2,1,0:T(8,128)(2,1)S(1)}, u32[]{:S(2)}, u32[]{:S(2)}) async-start(bf16[16,128,128]{2,1,0:T(8,128)(2,1)} %bitcast_bitcast_fusion), calls=%async_computation.2 | async-start | bytes 1048576 | tf_op jit(solution)/shard_map/all_to_all | solution.py:277
  51.1 0.8 copy-start.2
  58.2 19.4 %all-to-all-start.3 = ((bf16[16,128,128]{2,1,0:T(8,128)(2,1)}), bf16[16,128,128]{2,1,0:T(8,128)(2,1)S(1)}, u32[]{:S(2)}, u32[]{:S(2)}) async-start(bf16[16,128,128]{2,1,0:T(8,128)(2,1)} %bitcast.24), calls=%async_computation.3 | async-start | bytes 1048576 | tf_op jit(solution)/shard_map/all_to_all | solution.py:294
  77.6 0.8 copy-start.1
  84.2 14.2 %collective-permute-start = (bf16[128,2048]{1,0:T(8,128)(2,1)}, bf16[128,2048]{1,0:T(8,128)(2,1)S(1)}, u32[]{:S(2)}, u32[]{:S(2)}) collective-permute-start(bf16[128,2048]{1,0:T(8,128)(2,1)} %project_part.3), channel_id=1, source_target_pairs={{0,1},{1,0},{2,3},{3,2},{4,5},{5,4},{6,7},{7,6},{8,9},{9,8},{10,11... | collective-permute-start | bytes 1572872 | tf_op jit(solution)/shard_map/ppermute | solution.py:299

commit v2 on v0

--- a/solution.py
+++ b/solution.py
@@ -1,11 +1,15 @@
+import functools
 import math
 
 import jax
 import jax.numpy as jnp
 from jax import lax
+from jax.experimental import pallas as pl
+from jax.experimental.pallas import tpu as pltpu
 from jax.sharding import PartitionSpec as P
 
 BLOCK = 256
+MASKED = -1e30
 
 
 SELF_SCORE = -100000.0
@@ -69,7 +73,7 @@
     return jnp.where((rank_index >= 0)[..., None], rows, jnp.zeros((), rows.dtype))
 
 
-def local(shared_qk, values, buckets, counts, w_out):
+def local_by_bucket(shared_qk, values, buckets, counts, w_out):
     tok_rows = shared_qk.shape[0]
     head_count = buckets.shape[1]
     head_dim = shared_qk.shape[1] // head_count
@@ -151,6 +155,262 @@
     return projected.astype(jnp.bfloat16)
 
 
+PAD_ROWS = 8
+
+
+def in_vmem(count):
+    return [pl.BlockSpec(memory_space=pltpu.VMEM)] * count
+
+
+def in_hbm(count):
+    return [pl.BlockSpec(memory_space=pltpu.HBM)] * count
+
+
+def stays_in_hbm(array):
+    return pltpu.with_memory_space_constraint(array, pltpu.HBM)
+
+
+def vmem_params(mebibytes):
+    return pltpu.CompilerParams(vmem_limit_bytes=mebibytes * 2**20)
+
+
+def pack_kernel(bucket_hbm, qk_hbm, value_hbm, out_ref, bucket_ref, sems):
+    head_count, rows, head_dim = out_ref.shape
+    tok_rows = qk_hbm.shape[0]
+    copies = [pltpu.make_async_copy(bucket_hbm, bucket_ref, sems.at[2 * head_count])]
+    for head in range(head_count):
+        for which, source in enumerate((qk_hbm, value_hbm)):
+            copies.append(
+                pltpu.make_async_copy(
+                    source.at[:, head * head_dim : (head + 1) * head_dim],
+                    out_ref.at[head, which * tok_rows : (which + 1) * tok_rows, :],
+                    sems.at[2 * head + which],
+                )
+            )
+    for copy in copies:
+        copy.start()
+    copies[0].wait()
+    for head in range(head_count):
+        bucket = bucket_ref[head : head + 1, :].astype(jnp.float32)
+        out_ref[head, 2 * tok_rows :, :] = jnp.broadcast_to(bucket, (PAD_ROWS, tok_rows)).astype(out_ref.dtype)
+    for copy in copies[1:]:
+        copy.wait()
+
+
+def pack_heads(bucket_heads, shared_qk, values):
+    head_count, tok_rows = bucket_heads.shape
+    head_dim = shared_qk.shape[1] // head_count
+    return pl.pallas_call(
+        pack_kernel,
+        in_specs=in_hbm(3),
+        out_specs=in_vmem(1)[0],
+        out_shape=pltpu.VMEM((head_count, 2 * tok_rows + PAD_ROWS, head_dim), shared_qk.dtype),
+        scratch_shapes=[
+            pltpu.VMEM(bucket_heads.shape, bucket_heads.dtype),
+            pltpu.SemaphoreType.DMA((2 * head_count + 1,)),
+        ],
+        compiler_params=vmem_params(8),
+        name="pack_heads",
+    )(*(stays_in_hbm(array) for array in (bucket_heads, shared_qk, values)))
+
+
+def attend_kernel(
+    in_ref, w_hbm, out_ref, w_ref, query_ref, key_ref, value_ref, *scratch, bucket_count, query_rows
+):
+    source_count, tok_rows, head_dim = out_ref.shape
+    token_count = source_count * tok_rows
+    score_refs, term_refs, sem = scratch[:2], scratch[2:4], scratch[4]
+    width = w_ref.shape[1]
+    theirs = pl.multiple_of((1 - lax.axis_index("mp")) * width, width)
+    fetch = pltpu.make_async_copy(w_hbm.at[:, pl.ds(theirs, width)], w_ref, sem)
+    fetch.start()
+    lane = lax.broadcasted_iota(jnp.int32, (tok_rows, head_dim), 1)
+    for source in range(source_count):
+        at = slice(source * tok_rows, (source + 1) * tok_rows)
+        query_ref[at, :head_dim] = in_ref[source, :tok_rows, :]
+        key_ref[at, :head_dim] = in_ref[source, :tok_rows, :]
+        value_ref[at, :head_dim] = in_ref[source, tok_rows : 2 * tok_rows, :]
+        value_ref[at, head_dim:] = jnp.ones((tok_rows, head_dim), value_ref.dtype)
+        row = in_ref[source, 2 * tok_rows :, :].astype(jnp.float32)[:1]
+        bucket = jnp.broadcast_to(row, (head_dim, tok_rows)).T.astype(jnp.int32)
+        following = jnp.where(bucket == bucket_count - 1, 0, bucket + 1)
+        own = lane == bucket
+        query_ref[at, head_dim:] = jnp.where(own, 1.0, 0.0).astype(query_ref.dtype)
+        key_ref[at, head_dim:] = jnp.where(own | (lane == following), 0.0, MASKED).astype(key_ref.dtype)
+    scale = 1.0 / math.sqrt(head_dim)
+    strip = 16
+    square = (tok_rows, tok_rows)
+    itself = lax.broadcasted_iota(jnp.int32, square, 0) == lax.broadcasted_iota(jnp.int32, square, 1)
+
+    def scores_of(block, score_ref):
+        score_ref[...] = lax.dot_general(
+            query_ref[block * query_rows : (block + 1) * query_rows, :],
+            key_ref[...],
+            (((1,), (1,)), ((), ())),
+            preferred_element_type=jnp.float32,
+        )
+        for at in range(0, query_rows, tok_rows):
+            columns = slice(block * query_rows + at, block * query_rows + at + tok_rows)
+            own = score_ref[at : at + tok_rows, columns]
+            score_ref[at : at + tok_rows, columns] = jnp.where(itself, SELF_SCORE / scale, own)
+
+    def terms_of(score_ref, term_ref):
+        for at in range(0, query_rows, strip):
+            scores = score_ref[at : at + strip, :]
+            row_max = jnp.max(scores, axis=1, keepdims=True)
+            terms = jnp.exp2((scores - row_max) * (scale * math.log2(math.e)))
+            term_ref[at : at + strip, :] = terms.astype(term_ref.dtype)
+
+    def attend_of(block, term_ref):
+        both = jnp.dot(term_ref[...], value_ref[...], preferred_element_type=jnp.float32)
+        attended = (both[:, :head_dim] / both[:, head_dim:]).astype(out_ref.dtype)
+        for at in range(0, query_rows, tok_rows):
+            out_ref[(block * query_rows + at) // tok_rows] = attended[at : at + tok_rows]
+
+    blocks = token_count // query_rows
+    scores_of(0, score_refs[0])
+    for block in range(blocks):
+        if block + 1 < blocks:
+            scores_of(block + 1, score_refs[(block + 1) % 2])
+        terms_of(score_refs[block % 2], term_refs[block % 2])
+        attend_of(block, term_refs[block % 2])
+    fetch.wait()
+
+
+def attend_head(received, w_out, bucket_count):
+    source_count, rows, head_dim = received.shape
+    tok_rows = (rows - PAD_ROWS) // 2
+    token_count = source_count * tok_rows
+    query_rows = 2 * tok_rows
+    extended = pltpu.VMEM((token_count, 2 * head_dim), received.dtype)
+    scores = pltpu.VMEM((query_rows, token_count), jnp.float32)
+    terms = pltpu.VMEM((query_rows, token_count), received.dtype)
+    return pl.pallas_call(
+        functools.partial(attend_kernel, bucket_count=bucket_count, query_rows=query_rows),
+        in_specs=in_vmem(1) + in_hbm(1),
+        out_specs=tuple(in_vmem(2)),
+        out_shape=(
+            pltpu.VMEM((source_count, tok_rows, head_dim), received.dtype),
+            pltpu.VMEM((w_out.shape[0], w_out.shape[1] // 2), w_out.dtype),
+        ),
+        scratch_shapes=[
+            *(extended, extended, extended, scores, scores, terms, terms),
+            pltpu.SemaphoreType.DMA(()),
+        ],
+        compiler_params=vmem_params(20),
+        name="attend_head",
+    )(received, stays_in_hbm(w_out))
+
+
+def widen(token_ref, wide_ref):
+    head_count, tok_rows, head_dim = token_ref.shape
+    for head in range(head_count):
+        wide_ref[:, head * head_dim : (head + 1) * head_dim] = token_ref[head]
+
+
+def theirs_kernel(token_ref, w_ref, out_ref, wide_ref, *, chunk):
+    widen(token_ref, wide_ref)
+    columns = out_ref.shape[1]
+    out_ref[...] = jnp.dot(
+        wide_ref[...], w_ref[:, chunk * columns : (chunk + 1) * columns], preferred_element_type=jnp.float32
+    ).astype(out_ref.dtype)
+
+
+def project_theirs(token_heads, w_theirs, chunk, chunks):
+    head_count, tok_rows, head_dim = token_heads.shape
+    depth, features = w_theirs.shape
+    return pl.pallas_call(
+        functools.partial(theirs_kernel, chunk=chunk),
+        in_specs=in_vmem(2),
+        out_specs=in_vmem(1)[0],
+        out_shape=pltpu.VMEM((tok_rows, features // chunks), token_heads.dtype),
+        scratch_shapes=[pltpu.VMEM((tok_rows, depth), token_heads.dtype)],
+        compiler_params=vmem_params(16),
+        name="project_theirs",
+    )(token_heads, w_theirs)
+
+
+def ours_kernel(token_ref, w_hbm, out_ref, wide_ref, w_ref, sems):
+    chunks, depth, columns = w_ref.shape
+    start = pl.multiple_of(lax.axis_index("mp") * (chunks * columns), columns)
+    copies = [
+        pltpu.make_async_copy(w_hbm.at[:, pl.ds(start + chunk * columns, columns)], w_ref.at[chunk], sems.at[chunk])
+        for chunk in range(chunks)
+    ]
+    for copy in copies:
+        copy.start()
+    widen(token_ref, wide_ref)
+    for chunk, copy in enumerate(copies):
+        copy.wait()
+        out_ref[:, chunk * columns : (chunk + 1) * columns] = jnp.dot(
+            wide_ref[...], w_ref[chunk], preferred_element_type=jnp.float32
+        )
+
+
+def project_ours(token_heads, w_out):
+    head_count, tok_rows, head_dim = token_heads.shape
+    depth, features = w_out.shape
+    chunks = 4
+    columns = features // (2 * chunks)
+    return pl.pallas_call(
+        ours_kernel,
+        in_specs=in_vmem(1) + in_hbm(1),
+        out_specs=in_vmem(1)[0],
+        out_shape=pltpu.VMEM((tok_rows, chunks * columns), jnp.float32),
+        scratch_shapes=[
+            pltpu.VMEM((tok_rows, depth), token_heads.dtype),
+            pltpu.VMEM((chunks, depth, columns), w_out.dtype),
+            pltpu.SemaphoreType.DMA((chunks,)),
+        ],
+        compiler_params=vmem_params(20),
+        name="project_ours",
+    )(token_heads, stays_in_hbm(w_out))
+
+
+def add_kernel(ours_ref, *refs):
+    out_ref = refs[-1]
+    columns = refs[0].shape[1]
+    for chunk, theirs_ref in enumerate(refs[:-1]):
+        at = slice(chunk * columns, (chunk + 1) * columns)
+        out_ref[:, at] = (ours_ref[:, at] + theirs_ref[...].astype(jnp.float32)).astype(out_ref.dtype)
+
+
+def add_parts(ours, theirs, dtype):
+    return pl.pallas_call(
+        add_kernel,
+        in_specs=in_vmem(1 + len(theirs)),
+        out_shape=jax.ShapeDtypeStruct(ours.shape, dtype),
+        compiler_params=vmem_params(8),
+        name="add_parts",
+    )(ours, *theirs)
+
+
+def exchange(blocks):
+    return lax.all_to_all(blocks, "seq", split_axis=0, concat_axis=0, tiled=True)
+
+
+def local_by_head(shared_qk, values, buckets, counts, w_out):
+    received = exchange(pack_heads(buckets.T, shared_qk, values))
+    attended, w_theirs = attend_head(received, w_out, counts.shape[2])
+    token_heads = exchange(attended)
+    chunks = 2
+    arrived = [
+        lax.ppermute(project_theirs(token_heads, w_theirs, chunk, chunks), "mp", [(0, 1), (1, 0)])
+        for chunk in range(chunks)
+    ]
+    ours = project_ours(token_heads, w_out)
+    return add_parts(ours, arrived, shared_qk.dtype)
+
+
+def local(shared_qk, values, buckets, counts, w_out):
+    head_count = buckets.shape[1]
+    seq_count = lax.axis_size("seq")
+    one_head_each = head_count == seq_count and counts.shape[2] == seq_count and 2 < seq_count <= 128
+    if one_head_each and lax.axis_size("mp") == 2 and 2 * shared_qk.shape[0] <= BLOCK:
+        return local_by_head(shared_qk, values, buckets, counts, w_out)
+    return local_by_bucket(shared_qk, values, buckets, counts, w_out)
+
+
 def solution(mesh):
     placed = (P("seq", "mp"), P("seq", "mp"), P("seq", "mp"), P(None, "mp", None), P("mp", None))
     return jax.shard_map(

time: 402 us -> 75.3 us (0.19)
  local copies, waits for them, and re-layouts: 188 us -> 0 us
  waiting for transfers between devices: 126 us -> 7.13 us
  blocking collectives: 0 us -> 52.2 us
  matrix products: 35 us -> 0 us
  other arithmetic: 24.3 us -> 0 us
  between operations: 13.8 us -> 0.04 us
  Pallas kernels: 0 us -> 13.4 us
  starting transfers between devices: 12.4 us -> 2.15 us
    gather x7 -> x0, local copies, waits for them, and re-layouts: 168 us -> none  [the longest x1 45.3 us: owner_layout(): layout = received[source_dev, head_range[:, None], entry_row]]
    all_to_all x2 -> x0, waiting for transfers between devices: 62.4 us -> none  [the longest x1 40 us: local(): lax.all_to_all(outgoing, 'seq', split_axis=0, concat_axis=0, tiled=True)]
    all_to_all x0 -> x2, blocking collectives: none -> 52.2 us  [exchange(): lax.all_to_all(blocks, 'seq', split_axis=0, concat_axis=0, tiled=True)]
    dot_general x33 -> x0, matrix products: 35 us -> none  [the longest x16 19.3 us: block_attention(): jnp.einsum('cqd,ckd->cqk', queries, key_rows, preferred_element_type=jnp....]
    reduce_scatter x1 -> x0, waiting for transfers between devices: 34.2 us -> none  [local(): lax.psum_scatter(partial_sum, 'mp', scatter_dimension=1, tiled=True)]
    ppermute x1 -> x2, waiting for transfers between devices: 29.9 us -> 7.13 us  [local_by_head(): lax.ppermute(project_theirs(token_heads, w_theirs, chunk, chunks), 'mp',...]
    squeeze x16 -> x0, local copies, waits for them, and re-layouts: 15.5 us -> none  [local(): lax.map(lambda per_head: block_attention(per_head[0], per_head[1], per_he...]
    pallas_call x0 -> x6, Pallas kernels: none -> 13.4 us  [the longest x1 5.6 us: attend_head(): pl.pallas_call(functools.partial(attend_kernel, bucket_count=bucket_count...]
  transfers between devices with their start and end apart: 4 -> 2, of which waited for: 4 -> 2; matrix products, arithmetic and copies ran while one was open for 1% -> 0% of each run, Pallas kernels for 0% -> 6%
where the time goes in v2:
time: 75.3 us; the launch traced here: 75 us
  blocking collectives  52.2 us (69%)
  Pallas kernels  13.4 us (18%)
  waiting for transfers between devices  7.13 us (9%)
  starting transfers between devices  2.15 us (3%)
    all_to_all x2, blocking collectives, exchange(): lax.all_to_all(blocks, 'seq', split_axis=0, concat_axis=0, tiled=True)  52.2 us
    ppermute x2, waiting for transfers between devices, local_by_head(): lax.ppermute(project_theirs(token_heads, w_theirs, chunk, chunks), 'mp',...  7.13 us
    pallas_call x1, Pallas kernels, attend_head(): pl.pallas_call(functools.partial(attend_kernel, bucket_count=bucket_count...  5.6 us
    pallas_call x1, Pallas kernels, project_ours(): pl.pallas_call(ours_kernel, in_specs=in_vmem(1) + in_hbm(1), out_specs=in...  4.02 us
    ppermute x2, starting transfers between devices, local_by_head(): lax.ppermute(project_theirs(token_heads, w_theirs, chunk, chunks), 'mp',...  2.15 us
  transfers between devices with their start and end apart: 2, of which 2 were waited for; matrix products, arithmetic and copies ran while one was open for 0% of the time, Pallas kernels for 6%

profile of v2, /device:TPU:0, one launch (start us, length us, event | category | flops | bytes accessed | tf_op | source)
XLA Modules:
  0.0 75.0 jit_solution(129931738252713867)
XLA Ops:
  0.0 1.5 %pack_heads.1 = bf16[16,264,128]{2,1,0:T(8,128)(2,1)S(1)} custom-call(s32[16,128]{1,0:T(8,128)} %bitcast.1, bf16[128,2048]{1,0:T(8,128)(2,1)} %qk_hbm.1, bf16[128,2048]{1,0:T(8,128)(2,1)} %value_hbm.1), custom_call_target="tpu_custom_call" | custom-call | tf_op jit(solution)/shard_map/pack_heads/pallas_call | solution.py:203
  1.5 35.1 %all_to_all.10.in_ref = bf16[16,264,128]{2,1,0:T(8,128)(2,1)S(1)} all-to-all(bf16[16,264,128]{2,1,0:T(8,128)(2,1)S(1)} %pack_heads.1), channel_id=1, replica_groups=mesh['seq'=16,'mp'=2] {'seq'}, dimensions={0} | all-to-all | bytes 2162688 | tf_op jit(solution)/shard_map/all_to_all | solution.py:389
  36.6 5.6 %attend_head.1 = (bf16[16,128,128]{2,1,0:T(8,128)(2,1)S(1)}, bf16[2048,2048]{1,0:T(8,128)(2,1)S(1)}) custom-call(bf16[16,264,128]{2,1,0:T(8,128)(2,1)S(1)} %all_to_all.10.in_ref, bf16[2048,4096]{1,0:T(8,128)(2,1)} %w_hbm.3), custom_call_target="tpu_custom_call" | custom-call | tf_op jit(solution)/shard_map/attend_head/pallas_call | solution.py:288
  42.2 17.1 %all_to_all.11.token_ref = bf16[16,128,128]{2,1,0:T(8,128)(2,1)S(1)} all-to-all(bf16[16,128,128]{2,1,0:T(8,128)(2,1)S(1)} %get-tuple-element.7), channel_id=1, replica_groups=mesh['seq'=16,'mp'=2] {'seq'}, dimensions={0} | all-to-all | bytes 1048576 | tf_op jit(solution)/shard_map/all_to_all | solution.py:389
  59.3 0.7 project_theirs.2
  60.0 1.5 %collective-permute-start = (bf16[128,1024]{1,0:T(8,128)(2,1)S(1)}, bf16[128,1024]{1,0:T(8,128)(2,1)S(1)}, u32[]{:S(2)}, u32[]{:S(2)}) collective-permute-start(bf16[128,1024]{1,0:T(8,128)(2,1)S(1)} %project_theirs.2), channel_id=1, source_target_pairs={{0,1},{1,0},{2,3},{3,2},{4,5},{5,4},{6,7},{7,6},{8,9},{9,8},{10,11... | collective-permute-start | bytes 786440 | tf_op jit(solution)/shard_map/ppermute | solution.py:398
  61.6 0.7 project_theirs.3
  62.3 0.6 collective-permute-start.1
  62.9 4.0 %project_ours.1.ours_ref = f32[128,2048]{1,0:T(8,128)S(1)} custom-call(bf16[16,128,128]{2,1,0:T(8,128)(2,1)S(1)} %all_to_all.11.token_ref, bf16[2048,4096]{1,0:T(8,128)(2,1)} %w_hbm.3), custom_call_target="tpu_custom_call" | custom-call | tf_op jit(solution)/shard_map/project_ours/pallas_call | solution.py:355
  66.9 2.3 %collective-permute-done.refs_0_ = bf16[128,1024]{1,0:T(8,128)(2,1)S(1)} collective-permute-done((bf16[128,1024]{1,0:T(8,128)(2,1)S(1)}, bf16[128,1024]{1,0:T(8,128)(2,1)S(1)}, u32[]{:S(2)}, u32[]{:S(2)}) %collective-permute-start) | collective-permute-done | bytes 262176 | tf_op jit(solution)/shard_map/ppermute | solution.py:398
  69.3 4.8 %collective-permute-done.1.refs_1_ = bf16[128,1024]{1,0:T(8,128)(2,1)S(1)} collective-permute-done((bf16[128,1024]{1,0:T(8,128)(2,1)S(1)}, bf16[128,1024]{1,0:T(8,128)(2,1)S(1)}, u32[]{:S(2)}, u32[]{:S(2)}) %collective-permute-start.1) | collective-permute-done | bytes 262176 | tf_op jit(solution)/shard_map/ppermute | solution.py:398
  74.1 0.9 %add_parts.1 = bf16[128,2048]{1,0:T(8,128)(2,1)} custom-call(f32[128,2048]{1,0:T(8,128)S(1)} %project_ours.1.ours_ref, bf16[128,1024]{1,0:T(8,128)(2,1)S(1)} %collective-permute-done.refs_0_, bf16[128,1024]{1,0:T(8,128)(2,1)S(1)} %collective-permute-done.1.refs_1_), custom_call_target="tpu_custom_call" | custom-call | tf_op jit(solution)/shard_map/add_parts/pallas_call | solution.py:379
Async XLA Ops:
  60.0 9.2 %collective-permute-start = (bf16[128,1024]{1,0:T(8,128)(2,1)S(1)}, bf16[128,1024]{1,0:T(8,128)(2,1)S(1)}, u32[]{:S(2)}, u32[]{:S(2)}) collective-permute-start(bf16[128,1024]{1,0:T(8,128)(2,1)S(1)} %project_theirs.2), channel_id=1, source_target_pairs={{0,1},{1,0},{2,3},{3,2},{4,5},{5,4},{6,7},{7,6},{8,9},{9,8},{10,11... | collective-permute-start | bytes 786440 | tf_op jit(solution)/shard_map/ppermute | solution.py:398
  62.3 11.8 %collective-permute-start.1 = (bf16[128,1024]{1,0:T(8,128)(2,1)S(1)}, bf16[128,1024]{1,0:T(8,128)(2,1)S(1)}, u32[]{:S(2)}, u32[]{:S(2)}) collective-permute-start(bf16[128,1024]{1,0:T(8,128)(2,1)S(1)} %project_theirs.3), channel_id=1, source_target_pairs={{0,1},{1,0},{2,3},{3,2},{4,5},{5,4},{6,7},{7,6},{8,9},{9,8},{10,11... | collective-permute-start | bytes 786440 | tf_op jit(solution)/shard_map/ppermute | solution.py:398
